TPU v7x, 256 devices: a whole 4x4x8 slice. The times are simulated.
256 devices in a mesh: row: 8 (over x, core), col: 32 (over y, z).
Axes of the slice: x: 4, y: 4, z: 8, core: 2. Of those that a mesh axis runs over, the one named last changes fastest.
Arguments:
- src_coords: int32 [3, 131072], P(None, 'row'), may hold values from 0 to 51
- tgt_coords: int32 [3, 262144], P(None, 'col'), may hold values from 0 to 51
- src_mass: int32 [131072], P('row'), may hold values from 1 to 298
- tgt_mass: int32 [262144], P('col'), may hold values from 1 to 298
- tgt_start: float32 [262144], P('col'), may hold values from -10 to 170
- kept_src: int32 [8, 32, 64], P('row', 'col'), may hold values from 0 to 127, as said below
- kept_tgt: int32 [8, 32, 64], P('row', 'col'), may hold values from 0 to 63, as said below
- kept_count: int32 [8, 32], P('row', 'col'), may hold values from 1 to 64, as said below
Outputs:
- src_potential: float32 [131072], P('row')
- tgt_potential: float32 [262144], P('col')
Inputs may be any that keep to these rules, and one draw needn't show every extreme that they name: `kept_src`: every source tile lies in a live pair of some device of its row block. Slots at or past a device's count hold pairs that are not live. `kept_tgt`: every target tile lies in a live pair of some device of its column block. `kept_count`: some device has exactly 64 live slots in every draw.
All inputs are finite; a program needn't handle non-finite values.
Results may differ from a plain program's by a relative error of at most 0.0001.
Values sent between devices are 32-bit elements; how exact they have to be, the bound alone decides.
No kernel may reach another device: no remote copies, remote signals or barrier semaphores. Data moves between devices by JAX's collectives and lax.ppermute only.
A program may use at most 64 MiB of HBM per device.

v0:
```python
import jax
import jax.numpy as jnp
from jax import lax
from jax.sharding import PartitionSpec as P

ITERS = 3
very_negative = -1e30
cost_scale = 0.05


def tile_costs(src_coords, tgt_coords, src_ids, tgt_ids):
    src_tiles = jnp.take(src_coords.reshape(3, -1, 128), src_ids, axis=1).astype(jnp.float32)
    tgt_tiles = jnp.take(tgt_coords.reshape(3, -1, 128), tgt_ids, axis=1).astype(jnp.float32)
    square = None
    for component in range(3):
        difference = src_tiles[component][:, :, None] - tgt_tiles[component][:, None, :]
        square = difference * difference if component == 0 else square + difference * difference
    return cost_scale * square


def slot_partials(scores, live_slots, reduce_dim):
    peak_values = jnp.max(scores, axis=reduce_dim)
    totals = jnp.sum(jnp.exp(scores - jnp.expand_dims(peak_values, reduce_dim)), axis=reduce_dim)
    return (
        jnp.where(live_slots[:, None], peak_values, very_negative),
        jnp.where(live_slots[:, None], totals, 0.0),
    )


def fold_tiles(peak_values, totals, tile_ids, tile_count):
    member = tile_ids[:, None] == jnp.arange(tile_count, dtype=jnp.int32)[None, :]
    tile_peak = jnp.max(
        jnp.where(member[:, :, None], peak_values[:, None, :], very_negative), axis=0
    )
    slot_peak = jnp.take(tile_peak, tile_ids, axis=0)
    weighted = totals * jnp.exp(peak_values - slot_peak)
    tile_total = jnp.dot(member.astype(jnp.float32).T, weighted, precision=lax.Precision.HIGHEST)
    return (tile_peak.reshape(-1), tile_total.reshape(-1))


def row_merge(tile_peak, tile_total, src_log):
    highest = lax.pmax(tile_peak, "col")
    summed = lax.psum(tile_total * jnp.exp(tile_peak - highest), "col")
    return src_log - (highest + jnp.log(summed))


def col_merge(tile_peak, tile_total, tgt_log):
    highest = lax.pmax(tile_peak, "row")
    summed = lax.psum(tile_total * jnp.exp(tile_peak - highest), "row")
    return tgt_log - (highest + jnp.log(summed))


def on_device(
    src_coords, tgt_coords, src_mass, tgt_mass, tgt_start, kept_src, kept_tgt, kept_count
):
    src_ids = kept_src[0, 0]
    tgt_ids = kept_tgt[0, 0]
    live_slots = jnp.arange(src_ids.shape[0], dtype=jnp.int32) < kept_count[0, 0]
    src_tiles_count = src_coords.shape[1] // 128
    tgt_tiles_count = tgt_coords.shape[1] // 128
    src_weight = src_mass.astype(jnp.float32)
    tgt_weight = tgt_mass.astype(jnp.float32)
    src_sum = lax.psum(jnp.sum(src_weight), "row")
    tgt_sum = lax.psum(jnp.sum(tgt_weight), "col")
    src_log = jnp.log(src_weight) - jnp.log(src_sum)
    tgt_log = jnp.log(tgt_weight) - jnp.log(tgt_sum)
    cost = tile_costs(src_coords, tgt_coords, src_ids, tgt_ids)
    tgt_potential = tgt_start
    src_potential = None
    for iteration in range(ITERS):
        tgt_picked = jnp.take(tgt_potential.reshape(-1, 128), tgt_ids, axis=0)
        peak_values, totals = slot_partials(tgt_picked[:, None, :] - cost, live_slots, 2)
        tile_peak, tile_total = fold_tiles(peak_values, totals, src_ids, src_tiles_count)
        src_potential = row_merge(tile_peak, tile_total, src_log)
        src_picked = jnp.take(src_potential.reshape(-1, 128), src_ids, axis=0)
        peak_values, totals = slot_partials(src_picked[:, :, None] - cost, live_slots, 1)
        tile_peak, tile_total = fold_tiles(peak_values, totals, tgt_ids, tgt_tiles_count)
        tgt_potential = col_merge(tile_peak, tile_total, tgt_log)
    return (src_potential, tgt_potential)


def solution(mesh):
    placed = (
        P(None, "row"),
        P(None, "col"),
        P("row"),
        P("col"),
        P("col"),
        P("row", "col", None),
        P("row", "col", None),
        P("row", "col"),
    )
    return jax.shard_map(
        on_device, mesh=mesh, in_specs=placed, out_specs=(P("row"), P("col")), check_vma=False
    )
```

profile of v0, /device:TPU:8, one launch (start us, length us, event | category | flops | bytes accessed | tf_op | source)
XLA Modules:
  0.0 1064.5 jit_solution(4097321126829979318)
XLA Ops:
  7.2 0.7 compare_and_fusion
  7.9 0.7 fusion.61
  8.6 0.7 compare_select_fusion
  9.9 0.7 fusion.60
  10.6 0.7 compare_and_fusion.1
  11.2 0.7 gather_fusion
  12.1 0.7 copy-done.11
  12.8 0.7 gather_fusion.1
  13.7 0.5 copy-done.4
  14.2 0.6 gather_fusion.2
  15.0 5.1 subtract_reduce_fusion.5
  20.2 2.0 select_reduce_fusion.2
  22.3 6.4 exponential_reduce_fusion.5
  28.8 0.6 gather_fusion.3
  29.6 0.6 convert_reduce_fusion
  30.2 0.6 convert_reduce_fusion.1
  30.8 133.8 %all-reduce.7.cloned.1.call-done = f32[16384]{0:T(1024)} async-done(((f32[16384]{0:T(1024)}), f32[16384]{0:T(1024)}) %all-reduce.7.cloned.1.call-update) | async-done | bytes 65552 | tf_op jit(solution)/shard_map/pmax | solution.py:42
  164.6 1.9 fusion
  166.6 61.8 %psum.57 = f32[]{:T(128)} all-reduce(f32[]{:T(128)} %convert_reduce_fusion.1), channel_id=1, replica_groups=mesh['row'=8,'col'=32] {'col'}, use_global_device_ids=true, to_apply=%region_3.0 | all-reduce | flops 1 | bytes 8 | tf_op jit(solution)/shard_map/psum | solution.py:64
  228.4 13.1 %psum.56 = f32[]{:T(128)} all-reduce(f32[]{:T(128)} %convert_reduce_fusion), channel_id=1, replica_groups=mesh['row'=8,'col'=32] {'row'}, use_global_device_ids=true, to_apply=%region_1.0 | all-reduce | flops 1 | bytes 8 | tf_op jit(solution)/shard_map/psum | solution.py:63
  242.8 63.6 %all-reduce.9.cloned.1.call-done = f32[16384]{0:T(1024)} async-done(((f32[16384]{0:T(1024)}), f32[16384]{0:T(1024)}) %all-reduce.9.cloned.1.call-update) | async-done | bytes 65552 | tf_op jit(solution)/shard_map/psum | solution.py:43
  306.3 0.9 subtract_bitcast_fusion.1
  307.2 0.6 gather_fusion.4
  307.9 5.0 subtract_reduce_fusion.4
  312.9 5.1 exponential_reduce_fusion.4
  318.0 0.7 select_reduce_fusion.5
  318.7 0.6 gather_fusion.5
  319.3 23.6 %pmax.43 = f32[8192]{0:T(1024)S(1)} all-reduce(f32[8192]{0:T(1024)S(1)} %bitcast.78), channel_id=1, replica_groups=mesh['row'=8,'col'=32] {'row'}, use_global_device_ids=true, to_apply=%region_11.14 | all-reduce | flops 8192 | bytes 65536 | tf_op jit(solution)/shard_map/pmax | solution.py:48
  342.9 0.3 fusion.3
  343.2 23.6 %psum.59 = f32[8192]{0:T(1024)S(1)} all-reduce(f32[8192]{0:T(1024)S(1)} %fusion.3), channel_id=1, replica_groups=mesh['row'=8,'col'=32] {'row'}, use_global_device_ids=true, to_apply=%region_13.16 | all-reduce | flops 8192 | bytes 65536 | tf_op jit(solution)/shard_map/psum | solution.py:49
  366.8 0.6 gather_fusion.6
  367.5 5.1 subtract_reduce_fusion.3
  372.7 2.0 select_reduce_fusion.1
  374.8 6.4 exponential_reduce_fusion.3
  381.3 0.6 gather_fusion.7
  381.9 128.1 %all-reduce.11.cloned.1.call-done = f32[16384]{0:T(1024)} async-done(((f32[16384]{0:T(1024)}), f32[16384]{0:T(1024)}) %all-reduce.11.cloned.1.call-update) | async-done | bytes 65552 | tf_op jit(solution)/shard_map/pmax | solution.py:42
  510.0 1.9 fusion.1
  512.0 139.3 %all-reduce.13.cloned.1.call-done = f32[16384]{0:T(1024)} async-done(((f32[16384]{0:T(1024)}), f32[16384]{0:T(1024)}) %all-reduce.13.cloned.1.call-update) | async-done | bytes 65552 | tf_op jit(solution)/shard_map/psum | solution.py:43
  651.2 0.9 subtract_bitcast_fusion
  652.1 0.6 gather_fusion.8
  652.8 5.0 subtract_reduce_fusion.2
  657.7 5.1 exponential_reduce_fusion.2
  662.9 0.7 select_reduce_fusion.4
  663.6 0.6 gather_fusion.9
  664.2 23.6 %pmax.45 = f32[8192]{0:T(1024)S(1)} all-reduce(f32[8192]{0:T(1024)S(1)} %bitcast.79), channel_id=1, replica_groups=mesh['row'=8,'col'=32] {'row'}, use_global_device_ids=true, to_apply=%region_21.24 | all-reduce | flops 8192 | bytes 65536 | tf_op jit(solution)/shard_map/pmax | solution.py:48
  687.8 0.3 fusion.4
  688.1 23.6 %psum.61 = f32[8192]{0:T(1024)S(1)} all-reduce(f32[8192]{0:T(1024)S(1)} %fusion.4), channel_id=1, replica_groups=mesh['row'=8,'col'=32] {'row'}, use_global_device_ids=true, to_apply=%region_23.26 | all-reduce | flops 8192 | bytes 65536 | tf_op jit(solution)/shard_map/psum | solution.py:49
  711.7 0.6 gather_fusion.10
  712.4 5.1 subtract_reduce_fusion.1
  717.6 2.0 select_reduce_fusion
  719.9 6.4 exponential_reduce_fusion.1
  726.3 0.6 gather_fusion.11
  726.9 128.0 %all-reduce.15.cloned.1.call-done = f32[16384]{0:T(1024)} async-done(((f32[16384]{0:T(1024)}), f32[16384]{0:T(1024)}) %all-reduce.15.cloned.1.call-update) | async-done | bytes 65552 | tf_op jit(solution)/shard_map/pmax | solution.py:42
  854.9 1.9 fusion.2
  856.8 139.7 %all-reduce.17.cloned.1.call-done = f32[16384]{0:T(1024)} async-done(((f32[16384]{0:T(1024)}), f32[16384]{0:T(1024)}) %all-reduce.17.cloned.1.call-update) | async-done | bytes 65552 | tf_op jit(solution)/shard_map/psum | solution.py:43
  996.5 0.9 add_subtract_fusion
  997.4 0.6 gather_fusion.12
  998.1 5.0 subtract_reduce_fusion
  1003.1 5.1 exponential_reduce_fusion
  1008.2 0.7 select_reduce_fusion.3
  1008.9 0.6 gather_fusion.13
  1009.5 23.6 %pmax.47 = f32[8192]{0:T(1024)S(1)} all-reduce(f32[8192]{0:T(1024)S(1)} %bitcast.77), channel_id=1, replica_groups=mesh['row'=8,'col'=32] {'row'}, use_global_device_ids=true, to_apply=%region_31.34 | all-reduce | flops 8192 | bytes 65536 | tf_op jit(solution)/shard_map/pmax | solution.py:48
  1033.4 23.6 %psum.63 = f32[8192]{0:T(1024)S(1)} all-reduce(f32[8192]{0:T(1024)S(1)} %fusion.5), channel_id=1, replica_groups=mesh['row'=8,'col'=32] {'row'}, use_global_device_ids=true, to_apply=%region_33.36 | all-reduce | flops 8192 | bytes 65536 | tf_op jit(solution)/shard_map/psum | solution.py:49
  1057.0 0.6 add_subtract_fusion.1
  (64 shorter events, 2.6 us)
Async XLA Ops:
  7.2 4.1 copy-start
  7.2 157.4 %all-reduce.7.cloned.1.call-start = ((), (), s32[]{:S(2)}) async-start(), calls=%async_computation | async-start | bytes 131072 | tf_op jit(solution)/shard_map/pmax | solution.py:42
  11.9 0.9 copy-start.11
  13.5 0.8 copy-start.4
  13.6 1.3 copy-start.12
  22.2 6.5 copy-start.1
  22.3 284.1 %all-reduce.9.cloned.1.call-start = ((), (), s32[]{:S(2)}) async-start(), calls=%async_computation.1 | async-start | bytes 131072 | tf_op jit(solution)/shard_map/psum | solution.py:43
  28.7 0.8 copy-start.6
  28.7 1.4 copy-start.7
  29.6 136.9 %copy-start.13 = (s32[1,1,64]{2,1,0:T(1,128)S(1)}, s32[1,1,64]{2,1,0:T(1,128)}, u32[]{:S(2)}) copy-start(s32[1,1,64]{2,1,0:T(1,128)} %param.18) | copy-start | bytes 772
  164.6 141.8 %copy-start.8 = (f32[16384]{0:T(1024)S(1)}, f32[16384]{0:T(1024)}, u32[]{:S(2)}) copy-start(f32[16384]{0:T(1024)} %all-reduce.7.cloned.1.call-done) | copy-start | bytes 196612
  166.5 343.6 %all-reduce.11.cloned.1.call-start = ((), (), s32[]{:S(2)}) async-start(), calls=%async_computation.2 | async-start | bytes 131072 | tf_op jit(solution)/shard_map/pmax | solution.py:42
  374.8 6.5 copy-start.3
  374.8 276.4 %all-reduce.13.cloned.1.call-start = ((), (), s32[]{:S(2)}) async-start(), calls=%async_computation.3 | async-start | bytes 131072 | tf_op jit(solution)/shard_map/psum | solution.py:43
  510.0 141.2 %copy-start.9 = (f32[16384]{0:T(1024)S(1)}, f32[16384]{0:T(1024)}, u32[]{:S(2)}) copy-start(f32[16384]{0:T(1024)} %all-reduce.11.cloned.1.call-done) | copy-start | bytes 196612
  511.9 343.0 %all-reduce.15.cloned.1.call-start = ((), (), s32[]{:S(2)}) async-start(), calls=%async_computation.4 | async-start | bytes 131072 | tf_op jit(solution)/shard_map/pmax | solution.py:42
  719.7 6.7 copy-start.2
  719.7 276.8 %all-reduce.17.cloned.1.call-start = ((), (), s32[]{:S(2)}) async-start(), calls=%async_computation.5 | async-start | bytes 131072 | tf_op jit(solution)/shard_map/psum | solution.py:43
  854.9 141.6 %copy-start.10 = (f32[16384]{0:T(1024)S(1)}, f32[16384]{0:T(1024)}, u32[]{:S(2)}) copy-start(f32[16384]{0:T(1024)} %all-reduce.15.cloned.1.call-done) | copy-start | bytes 196612
  997.4 5.7 copy-start.5
Sparse Core Ops, SparseCore 0:
  22.4 142.1 all-reduce.6
  169.0 137.2 all-reduce.8
  374.9 135.0 all-reduce.10
  513.9 137.2 all-reduce.12
  719.8 135.0 all-reduce.14
  859.2 137.2 all-reduce.16
where the time goes:
time: 1070 us; the launch traced here: 1060 us
  waiting for transfers between devices  733 us (69%)
  blocking collectives  216 us (20%)
  other arithmetic  82.2 us (8%)
  between operations  16.4 us (2%)
    pmax x3, waiting for transfers between devices, row_merge(): highest = lax.pmax(tile_peak, 'col')  390 us
    psum x3, waiting for transfers between devices, row_merge(): summed = lax.psum(tile_total * jnp.exp(tile_peak - highest), 'col')  343 us
    psum x3, blocking collectives, col_merge(): summed = lax.psum(tile_total * jnp.exp(tile_peak - highest), 'row')  70.8 us
    pmax x3, blocking collectives, col_merge(): highest = lax.pmax(tile_peak, 'row')  70.8 us
    psum x1, blocking collectives, on_device(): tgt_sum = lax.psum(jnp.sum(tgt_weight), 'col')  61.8 us
    reduce_sum x6, other arithmetic, slot_partials(): jnp.sum(jnp.exp(scores - jnp.expand_dims(peak_values, reduce_dim)), axis=...  34.4 us
    reduce_max x6, other arithmetic, slot_partials(): peak_values = jnp.max(scores, axis=reduce_dim)  30.4 us
  transfers between devices with their start and end apart: 6, of which 6 were waited for; matrix products, arithmetic and copies ran while one was open for 2% of the time, Pallas kernels for 0%

commit v1 on v0

--- a/solution.py
+++ b/solution.py
@@ -40,7 +40,7 @@
 
 def row_merge(tile_peak, tile_total, src_log):
     highest = lax.pmax(tile_peak, "col")
-    summed = lax.psum(tile_total * jnp.exp(tile_peak - highest), "col")
+    summed = jnp.sum(lax.all_gather(tile_total * jnp.exp(tile_peak - highest), "col"), axis=0)
     return src_log - (highest + jnp.log(summed))
 
 

time: 1070 us -> 890 us (0.83)
  waiting for transfers between devices: 733 us -> 551 us
    psum x3 -> x0, waiting for transfers between devices: 343 us -> none  [row_merge(): summed = lax.psum(tile_total * jnp.exp(tile_peak - highest), 'col')]
    all_gather x0 -> x3, waiting for transfers between devices: none -> 153 us  [row_merge(): lax.all_gather(tile_total * jnp.exp(tile_peak - highest), 'col')]
  transfers between devices with their start and end apart: 6 -> 6, of which waited for: 6 -> 5; matrix products, arithmetic and copies ran while one was open for 2% -> 3% of each run, Pallas kernels for 0% -> 0%
where the time goes in v1:
time: 890 us; the launch traced here: 889 us
  waiting for transfers between devices  551 us (62%)
  blocking collectives  217 us (24%)
  other arithmetic  81 us (9%)
  local copies, waits for them, and re-layouts  17.5 us (2%)
  between operations  16.5 us (2%)
    pmax x3, waiting for transfers between devices, row_merge(): highest = lax.pmax(tile_peak, 'col')  398 us
    all_gather x3, waiting for transfers between devices, row_merge(): lax.all_gather(tile_total * jnp.exp(tile_peak - highest), 'col')  153 us
    psum x3, blocking collectives, col_merge(): summed = lax.psum(tile_total * jnp.exp(tile_peak - highest), 'row')  71 us
    pmax x3, blocking collectives, col_merge(): highest = lax.pmax(tile_peak, 'row')  70.8 us
    psum x1, blocking collectives, on_device(): tgt_sum = lax.psum(jnp.sum(tgt_weight), 'col')  61.9 us
    reduce_sum x6, other arithmetic, slot_partials(): jnp.sum(jnp.exp(scores - jnp.expand_dims(peak_values, reduce_dim)), axis=...  34.5 us
    reduce_max x6, other arithmetic, slot_partials(): peak_values = jnp.max(scores, axis=reduce_dim)  30.4 us
  transfers between devices with their start and end apart: 6, of which 5 were waited for; matrix products, arithmetic and copies ran while one was open for 3% of the time, Pallas kernels for 0%

profile of v1, /device:TPU:8, one launch (start us, length us, event | category | flops | bytes accessed | tf_op | source)
XLA Modules:
  0.0 889.3 jit_solution(5867446443278503430)
XLA Ops:
  7.2 0.7 compare_and_fusion
  7.9 0.7 compare_select_fusion
  8.6 0.7 fusion.61
  9.9 0.7 fusion.60
  10.6 0.7 compare_and_fusion.1
  11.3 0.7 iota_compare_fusion.1
  12.0 0.7 gather_fusion
  12.9 1.4 gather_fusion.2
  14.4 1.6 gather_fusion.1
  16.2 5.1 subtract_reduce_fusion.5
  21.4 2.0 select_reduce_fusion.2
  23.5 6.4 exponential_reduce_fusion.5
  30.0 0.6 gather_fusion.3
  30.6 135.1 %all-reduce.4.cloned.1.call-done = f32[16384]{0:T(1024)} async-done(((f32[16384]{0:T(1024)}), f32[16384]{0:T(1024)}) %all-reduce.4.cloned.1.call-update) | async-done | bytes 65552 | tf_op jit(solution)/shard_map/pmax | solution.py:42
  165.7 1.8 fusion
  167.6 0.7 convert_reduce_fusion.1
  168.3 0.6 convert_reduce_fusion
  168.9 61.9 %psum.36 = f32[]{:T(128)} all-reduce(f32[]{:T(128)} %convert_reduce_fusion.1), channel_id=1, replica_groups=mesh['row'=8,'col'=32] {'col'}, use_global_device_ids=true, to_apply=%region_3.0 | all-reduce | flops 1 | bytes 8 | tf_op jit(solution)/shard_map/psum | solution.py:64
  230.8 13.3 %psum.35 = f32[]{:T(128)} all-reduce(f32[]{:T(128)} %convert_reduce_fusion), channel_id=1, replica_groups=mesh['row'=8,'col'=32] {'row'}, use_global_device_ids=true, to_apply=%region_1.0 | all-reduce | flops 1 | bytes 8 | tf_op jit(solution)/shard_map/psum | solution.py:63
  245.5 1.8 reshape.428
  247.5 0.6 copy-done.7
  248.1 0.6 gather_fusion.4
  248.8 5.0 subtract_reduce_fusion.4
  253.8 5.1 exponential_reduce_fusion.4
  258.9 0.7 select_reduce_fusion.5
  259.7 0.6 gather_fusion.5
  260.3 23.6 %pmax.43 = f32[8192]{0:T(1024)S(1)} all-reduce(f32[8192]{0:T(1024)S(1)} %bitcast.78), channel_id=1, replica_groups=mesh['row'=8,'col'=32] {'row'}, use_global_device_ids=true, to_apply=%region_11.14 | all-reduce | flops 8192 | bytes 65536 | tf_op jit(solution)/shard_map/pmax | solution.py:48
  283.9 0.3 fusion.3
  284.1 23.6 %psum.37 = f32[8192]{0:T(1024)S(1)} all-reduce(f32[8192]{0:T(1024)S(1)} %fusion.3), channel_id=1, replica_groups=mesh['row'=8,'col'=32] {'row'}, use_global_device_ids=true, to_apply=%region_13.16 | all-reduce | flops 8192 | bytes 65536 | tf_op jit(solution)/shard_map/psum | solution.py:49
  307.8 0.6 gather_fusion.6
  308.4 5.1 subtract_reduce_fusion.3
  313.7 2.0 select_reduce_fusion.1
  315.8 6.4 exponential_reduce_fusion.3
  322.2 0.6 gather_fusion.7
  322.8 134.6 %all-reduce.6.cloned.1.call-done = f32[16384]{0:T(1024)} async-done(((f32[16384]{0:T(1024)}), f32[16384]{0:T(1024)}) %all-reduce.6.cloned.1.call-update) | async-done | bytes 65552 | tf_op jit(solution)/shard_map/pmax | solution.py:42
  457.4 1.8 fusion.1
  459.2 76.2 %all-gather.9.cloned.1.call-done = f32[524288]{0:T(1024)} async-done(((f32[16384]{0:T(1024)}), f32[524288]{0:T(1024)}) %all-gather.9.cloned.1.call-update) | async-done | bytes 2097168 | tf_op jit(solution)/shard_map/all_gather | solution.py:43
  535.5 1.7 reshape.429
  537.5 0.6 copy-done.8
  538.1 0.6 gather_fusion.8
  538.8 5.0 subtract_reduce_fusion.2
  543.8 5.1 exponential_reduce_fusion.2
  548.9 0.7 select_reduce_fusion.4
  549.6 0.6 gather_fusion.9
  550.2 23.6 %pmax.45 = f32[8192]{0:T(1024)S(1)} all-reduce(f32[8192]{0:T(1024)S(1)} %bitcast.79), channel_id=1, replica_groups=mesh['row'=8,'col'=32] {'row'}, use_global_device_ids=true, to_apply=%region_21.24 | all-reduce | flops 8192 | bytes 65536 | tf_op jit(solution)/shard_map/pmax | solution.py:48
  574.1 23.8 %psum.38 = f32[8192]{0:T(1024)S(1)} all-reduce(f32[8192]{0:T(1024)S(1)} %fusion.4), channel_id=1, replica_groups=mesh['row'=8,'col'=32] {'row'}, use_global_device_ids=true, to_apply=%region_23.26 | all-reduce | flops 8192 | bytes 65536 | tf_op jit(solution)/shard_map/psum | solution.py:49
  597.9 0.6 gather_fusion.10
  598.6 5.1 subtract_reduce_fusion.1
  603.8 2.0 select_reduce_fusion
  605.9 6.4 exponential_reduce_fusion.1
  612.4 0.6 gather_fusion.11
  613.0 128.2 %all-reduce.8.cloned.1.call-done = f32[16384]{0:T(1024)} async-done(((f32[16384]{0:T(1024)}), f32[16384]{0:T(1024)}) %all-reduce.8.cloned.1.call-update) | async-done | bytes 65552 | tf_op jit(solution)/shard_map/pmax | solution.py:42
  741.1 1.8 fusion.2
  742.9 76.6 %all-gather.11.cloned.1.call-done = f32[524288]{0:T(1024)} async-done(((f32[16384]{0:T(1024)}), f32[524288]{0:T(1024)}) %all-gather.11.cloned.1.call-update) | async-done | bytes 2097168 | tf_op jit(solution)/shard_map/all_gather | solution.py:43
  819.6 1.7 reshape.430
  821.5 0.6 copy-done.9
  822.2 0.6 gather_fusion.12
  822.9 5.0 subtract_reduce_fusion
  827.9 5.1 exponential_reduce_fusion
  833.0 0.7 select_reduce_fusion.3
  833.7 0.6 gather_fusion.13
  834.3 23.6 %pmax.47 = f32[8192]{0:T(1024)S(1)} all-reduce(f32[8192]{0:T(1024)S(1)} %bitcast.77), channel_id=1, replica_groups=mesh['row'=8,'col'=32] {'row'}, use_global_device_ids=true, to_apply=%region_31.34 | all-reduce | flops 8192 | bytes 65536 | tf_op jit(solution)/shard_map/pmax | solution.py:48
  858.2 23.6 %psum.39 = f32[8192]{0:T(1024)S(1)} all-reduce(f32[8192]{0:T(1024)S(1)} %fusion.5), channel_id=1, replica_groups=mesh['row'=8,'col'=32] {'row'}, use_global_device_ids=true, to_apply=%region_33.36 | all-reduce | flops 8192 | bytes 65536 | tf_op jit(solution)/shard_map/psum | solution.py:49
  881.8 0.6 add_subtract_fusion.1
  (66 shorter events, 3.1 us)
Async XLA Ops:
  7.2 4.8 copy-start
  7.2 16.3 %copy-start.10 = (s32[1,1,64]{2,1,0:T(1,128)S(1)}, s32[1,1,64]{2,1,0:T(1,128)}, u32[]{:S(2)}) copy-start(s32[1,1,64]{2,1,0:T(1,128)} %param.17) | copy-start | bytes 772
  7.2 158.5 %all-reduce.4.cloned.1.call-start = ((), (), s32[]{:S(2)}) async-start(), calls=%async_computation | async-start | bytes 131072 | tf_op jit(solution)/shard_map/pmax | solution.py:42
  12.9 154.7 %copy-start.6 = (s32[8192]{0:T(1024)S(1)}, s32[8192]{0:T(1024)}, u32[]{:S(2)}) copy-start(s32[8192]{0:T(1024)} %param.15) | copy-start | bytes 98308
  12.9 155.4 %copy-start.5 = (s32[16384]{0:T(1024)S(1)}, s32[16384]{0:T(1024)}, u32[]{:S(2)}) copy-start(s32[16384]{0:T(1024)} %param.14) | copy-start | bytes 196612
  12.9 232.5 %copy-start.11 = (s32[1,1,64]{2,1,0:T(1,128)S(1)}, s32[1,1,64]{2,1,0:T(1,128)}, u32[]{:S(2)}) copy-start(s32[1,1,64]{2,1,0:T(1,128)} %param.18) | copy-start | bytes 772
  23.4 6.5 copy-start.1
  23.5 222.0 %all-gather.7.cloned.1.call-start = ((), (), s32[]{:S(2)}) async-start(), calls=%async_computation.3 | async-start | bytes 2162688 | tf_op jit(solution)/shard_map/all_gather | solution.py:43
  167.5 289.8 %all-reduce.6.cloned.1.call-start = ((), (), s32[]{:S(2)}) async-start(), calls=%async_computation.1 | async-start | bytes 131072 | tf_op jit(solution)/shard_map/pmax | solution.py:42
  247.3 0.8 copy-start.7
  315.7 6.5 copy-start.3
  315.7 219.8 %all-gather.9.cloned.1.call-start = ((), (), s32[]{:S(2)}) async-start(), calls=%async_computation.4 | async-start | bytes 2162688 | tf_op jit(solution)/shard_map/all_gather | solution.py:43
  459.2 281.9 %all-reduce.8.cloned.1.call-start = ((), (), s32[]{:S(2)}) async-start(), calls=%async_computation.2 | async-start | bytes 131072 | tf_op jit(solution)/shard_map/pmax | solution.py:42
  537.2 0.8 copy-start.8
  605.8 6.5 copy-start.2
  605.9 213.7 %all-gather.11.cloned.1.call-start = ((), (), s32[]{:S(2)}) async-start(), calls=%async_computation.5 | async-start | bytes 2162688 | tf_op jit(solution)/shard_map/all_gather | solution.py:43
  821.3 0.8 copy-start.9
  822.2 60.3 %copy-start.4 = (f32[16384]{0:T(1024)}, f32[16384]{0:T(1024)S(1)}, u32[]{:S(2)}) copy-start(f32[16384]{0:T(1024)S(1)} %add_subtract_fusion) | copy-start | bytes 196612
Sparse Core Ops, SparseCore 0:
  23.6 142.0 all-reduce.3
  169.2 75.0 all-gather.6
  315.8 141.4 all-reduce.5
  460.4 75.0 all-gather.8
  606.0 135.0 all-reduce.7
  744.5 75.0 all-gather.10
